TPU v7x, 32 devices: a whole 2x2x4 slice. The times are simulated.
32 devices in a mesh: groups: 2 (over y), frame: 4 (over z), panel: 2 (over x), sub: 2 (over core).
Axes of the slice: x: 2, y: 2, z: 4, core: 2. Of those that a mesh axis runs over, the one named last changes fastest.
Arguments:
- frames: bfloat16 [2048, 65536], P(('groups', 'frame'), ('panel', 'sub')), parts along dimension 0, may hold values from -16 to 16
- slices: float32 [32, 65536], P(('groups', 'frame'), ('panel', 'sub')), parts along dimension 0, may hold values from -8 to 8
- log_prior: float32 [4096], replicated, may hold values from -2 to 2
- orient: int32 [32], P('groups'), parts along dimension 0, may hold values from 0 to 4095
Outputs:
- new_slices: float32 [32, 65536], P(('groups', 'frame'), ('panel', 'sub')), parts along dimension 0
There are 2 independent parts, one for each index of `groups`. A program takes and returns all parts, laid end to end along the dimension named above; an argument that names none is the same for every part. Nothing has to cross between parts.
All inputs are finite; a program needn't handle non-finite values.
Results may differ from a plain program's by a relative error of at most 0.022.
The roundings to bfloat16 on the way count: a program that leaves them out, or rounds other values in their place, can miss the bound.
Values may be sent and summed in bfloat16 or wider, within the bound.
A program may use at most 64 MiB of HBM per device.

v0:
```python
import math

import jax
import jax.numpy as jnp
from jax import lax
from jax.sharding import PartitionSpec as P

PIX = 65536
ITERS = 2


def fetch_slices(owned_b):
    return lax.all_gather(owned_b, "frame", axis=0, tiled=True)


def owner_update(weights, frames, counts, owned_b, offset):
    owned = owned_b.shape[0]
    mine = lax.psum_scatter(
        jnp.einsum("fm,fp->mp", weights, frames, preferred_element_type=jnp.float32).astype(
            jnp.bfloat16
        ),
        "frame",
        scatter_dimension=0,
        tiled=True,
    ).astype(jnp.float32)
    my_counts = lax.dynamic_slice_in_dim(counts, offset, owned, 0)
    return (mine + owned_b.astype(jnp.float32)) / (my_counts + 1.0)[:, None]


def local(frames, slices, log_prior, orient):
    owned = slices.shape[0]
    temper = 3.0 / math.sqrt(PIX)
    matches = orient[:, None] == jnp.arange(log_prior.shape[0], dtype=jnp.int32)[None, :]
    prior = jnp.sum(jnp.where(matches, log_prior[None, :], 0.0), axis=1)
    offset = lax.axis_index("frame") * owned
    current = slices
    owned_b = slices.astype(jnp.bfloat16)
    for step in range(ITERS):
        if step == 0:
            gathered = fetch_slices(owned_b)
        else:
            gathered = fetch_slices(owned_b)
        wide = gathered.astype(jnp.float32)
        norms = jnp.sum(wide * wide, axis=1)
        raw = (
            jnp.einsum("fp,mp->fm", frames, gathered, preferred_element_type=jnp.float32)
            - 0.5 * norms[None, :]
        )
        summed = lax.psum(raw, ("panel", "sub"))
        weights = jax.nn.softmax(temper * summed + prior[None, :], axis=1).astype(jnp.bfloat16)
        counts = lax.psum(jnp.sum(weights.astype(jnp.float32), axis=0), "frame")
        if step + 1 < ITERS:
            current = owner_update(weights, frames, counts, owned_b, offset)
            owned_b = current.astype(jnp.bfloat16)
        else:
            current = owner_update(weights, frames, counts, owned_b, offset)
    return current


def solution(mesh):
    in_specs = (
        P(("groups", "frame"), ("panel", "sub")),
        P(("groups", "frame"), ("panel", "sub")),
        P(),
        P("groups"),
    )
    out_specs = P(("groups", "frame"), ("panel", "sub"))
    return jax.shard_map(local, mesh=mesh, in_specs=in_specs, out_specs=out_specs, check_vma=False)
```

profile of v0, /device:TPU:0, one launch (start us, length us, event | category | flops | bytes accessed | tf_op | source)
XLA Modules:
  0.0 173.9 jit_solution(4613914813418080331)
XLA Ops:
  6.5 1.0 convert_bitcast_fusion
  7.6 17.4 %all-gather = bf16[4,4,16384]{2,1,0:T(4,128)(2,1)S(1)} all-gather(bf16[1,4,16384]{2,1,0:T(4,128)(2,1)S(1)} %convert_bitcast_fusion), channel_id=1, replica_groups=mesh['groups'=2,'frame'=4,'panel'=2,'sub'=2] {'frame'}, dimensions={0}, use_global_device_ids=true | all-gather | bytes 655360 | tf_op jit(solution)/shard_map/all_gather | solution.py:13
  24.9 0.1 reshape.18
  25.1 0.2 multiply_reduce_fusion.1
  25.3 5.7 %convolution_subtract_fusion.1 = f32[256,16]{0,1:T(8,128)S(1)} fusion(bf16[256,16384]{1,0:T(8,128)(2,1)} %param.4, bf16[16,16384]{1,0:T(8,128)(2,1)S(1)} %reshape.18, f32[16]{0:T(128)S(1)} %broadcast_multiply_fusion.1), kind=kOutput, calls=%fused_computation.4 | convolution fusion | flops 134221824 | bytes 8929344 | tf_op jit(solution)/shard_map/fp,mp->fm/dot_general | solution.py:46
  31.0 10.1 %psum.28 = f32[256,16]{0,1:T(8,128)S(1)} all-reduce(f32[256,16]{0,1:T(8,128)S(1)} %convolution_subtract_fusion.1), channel_id=1, replica_groups=mesh['groups'=2,'frame'=4,'panel'=2,'sub'=2] {'panel','sub'}, use_global_device_ids=true, to_apply=%region_1.2 | all-reduce | flops 4096 | bytes 32768 | tf_op jit(solution)/shard_map/psum | solution.py:49
  41.1 0.2 select_reduce_fusion
  41.5 0.1 fusion.4
  41.6 0.2 convert_reduce_fusion.1
  41.7 5.4 %convolution_convert_fusion.1 = bf16[16,16384]{1,0:T(8,128)(2,1)} fusion(bf16[256,16]{0,1:T(8,128)(2,1)S(1)} %get-tuple-element.8, bf16[256,16384]{1,0:T(8,128)(2,1)} %param.4), kind=kOutput, calls=%fused_computation.1 | convolution fusion | flops 134479872 | bytes 8921088 | tf_op jit(solution)/shard_map/fm,fp->mp/dot_general | solution.py:19
  47.3 0.6 dynamic-slice
  48.5 12.6 %psum.29 = f32[16]{0:T(128)S(1)} all-reduce(f32[16]{0:T(128)S(1)} %get-tuple-element.7), channel_id=1, replica_groups=mesh['groups'=2,'frame'=4,'panel'=2,'sub'=2] {'frame'}, use_global_device_ids=true, to_apply=%region_7.8 | all-reduce | flops 16 | bytes 128 | tf_op jit(solution)/shard_map/psum | solution.py:51
  61.1 26.4 %all-reduce.5.cloned.1.call-done = bf16[16,16384]{1,0:T(8,128)(2,1)} async-done(((bf16[16,16384]{1,0:T(8,128)(2,1)}), bf16[16,16384]{1,0:T(8,128)(2,1)}) %all-reduce.5.cloned.1.call-update) | async-done | bytes 524304
  87.6 1.1 fusion.1
  88.6 16.2 %all-gather.1 = bf16[4,4,16384]{2,1,0:T(4,128)(2,1)S(1)} all-gather(bf16[1,4,16384]{2,1,0:T(4,128)(2,1)S(1)} %bitcast.14), channel_id=1, replica_groups=mesh['groups'=2,'frame'=4,'panel'=2,'sub'=2] {'frame'}, dimensions={0}, use_global_device_ids=true | all-gather | bytes 655360 | tf_op jit(solution)/shard_map/all_gather | solution.py:13
  104.8 0.1 reshape.20
  104.9 0.2 multiply_reduce_fusion
  105.2 5.6 %fusion = f32[256,16]{0,1:T(8,128)S(1)} fusion(bf16[16,16384]{1,0:T(8,128)(2,1)S(1)} %reshape.20, bf16[256,16384]{1,0:T(8,128)(2,1)} %param.4, f32[16]{0:T(128)S(1)} %broadcast_multiply_fusion), kind=kOutput, calls=%fused_computation.3 | convolution fusion | flops 134221824 | bytes 8929344 | tf_op jit(solution)/shard_map/fp,mp->fm/dot_general | solution.py:46
  110.8 10.1 %psum.30 = f32[256,16]{0,1:T(8,128)S(1)} all-reduce(f32[256,16]{0,1:T(8,128)S(1)} %fusion), channel_id=1, replica_groups=mesh['groups'=2,'frame'=4,'panel'=2,'sub'=2] {'panel','sub'}, use_global_device_ids=true, to_apply=%region_9.10 | all-reduce | flops 4096 | bytes 32768 | tf_op jit(solution)/shard_map/psum | solution.py:49
  121.1 0.2 convert_reduce_fusion
  121.3 5.4 %convolution_convert_fusion = bf16[16,16384]{1,0:T(8,128)(2,1)} fusion(bf16[256,16]{0,1:T(8,128)(2,1)S(1)} %get-tuple-element.6, bf16[256,16384]{1,0:T(8,128)(2,1)} %param.4), kind=kOutput, calls=%fused_computation | convolution fusion | flops 134479872 | bytes 8921088 | tf_op jit(solution)/shard_map/fm,fp->mp/dot_general | solution.py:19
  126.7 10.8 %psum.31 = f32[16]{0:T(128)S(1)} all-reduce(f32[16]{0:T(128)S(1)} %get-tuple-element.5), channel_id=1, replica_groups=mesh['groups'=2,'frame'=4,'panel'=2,'sub'=2] {'frame'}, use_global_device_ids=true, to_apply=%region_14.15 | all-reduce | flops 16 | bytes 128 | tf_op jit(solution)/shard_map/psum | solution.py:51
  137.6 27.7 %all-reduce.7.cloned.1.call-done = bf16[16,16384]{1,0:T(8,128)(2,1)} async-done(((bf16[16,16384]{1,0:T(8,128)(2,1)}), bf16[16,16384]{1,0:T(8,128)(2,1)}) %all-reduce.7.cloned.1.call-update) | async-done | bytes 524304
  165.3 1.8 %add_divide_fusion = f32[4,16384]{1,0:T(4,128)} fusion(bf16[4,16384]{1,0:T(4,128)(2,1)S(1)} %fusion.1, bf16[16,16384]{1,0:T(8,128)(2,1)} %all-reduce.7.cloned.1.call-done, u32[]{:T(128)S(6)} %multiply.1, f32[4]{0:T(128)S(1)} %dynamic-slice_add_fusion), kind=kLoop, calls=%fused_computation.7 | loop fusion | flops 262144 | bytes 524308 | tf_op jit(solution)/shard_map/div | solution.py:27
  (19 shorter events, 0.5 us)
Async XLA Ops:
  6.5 34.6 %copy-start.2 = (s32[16]{0:T(128)S(1)}, s32[16]{0:T(128)}, u32[]{:S(2)}) copy-start(s32[16]{0:T(128)} %param.7) | copy-start | bytes 196
  6.5 34.6 %copy-start.1 = (f32[4096]{0:T(1024)S(1)}, f32[4096]{0:T(1024)}, u32[]{:S(2)}) copy-start(f32[4096]{0:T(1024)} %param.6) | copy-start | bytes 49156
  6.5 81.0 %all-reduce.5.cloned.1.call-start = ((), (), s32[]{:S(2)}) async-start(), calls=%async_computation | async-start | bytes 1048576
  25.3 21.9 %copy-start.3 = (u32[32]{0:T(128)S(1)}, u32[32]{0:T(128)}, u32[]{:S(2)}) copy-start(u32[32]{0:T(128)} %constant.25) | copy-start | bytes 388
  25.3 62.2 %copy-start = (f32[4,16384]{1,0:T(4,128)S(1)}, f32[4,16384]{1,0:T(4,128)}, u32[]{:S(2)}) copy-start(f32[4,16384]{1,0:T(4,128)} %param.5) | copy-start | bytes 786436
  47.2 118.2 %all-reduce.7.cloned.1.call-start = ((), (), s32[]{:S(2)}) async-start(), calls=%async_computation.1 | async-start | bytes 1048576
Sparse Core Ops, SparseCore 0:
  47.3 40.1 all-reduce.4
  126.9 38.4 all-reduce.6
where the time goes:
time: 174 us
  blocking collectives  77.1 us (44%)
  waiting for transfers between devices  54.2 us (31%)
  matrix products  22.2 us (13%)
  between operations  14.1 us (8%)
  other arithmetic  5.48 us (3%)
    unnamed x4, waiting for transfers between devices  54.2 us
    all_gather x2, blocking collectives, fetch_slices(): return lax.all_gather(owned_b, 'frame', axis=0, tiled=True)  33.5 us
    psum x2, blocking collectives, local(): counts = lax.psum(jnp.sum(weights.astype(jnp.float32), axis=0), 'frame')  23.3 us
    psum x2, blocking collectives, local(): summed = lax.psum(raw, ('panel', 'sub'))  20.2 us
    dot_general x2, matrix products, local(): jnp.einsum('fp,mp->fm', frames, gathered, preferred_element_type=jnp.floa...  11.3 us
    dot_general x2, matrix products, owner_update(): jnp.einsum('fm,fp->mp', weights, frames, preferred_element_type=jnp.float32)  10.8 us
  transfers between devices with their start and end apart: 2, of which 2 were waited for; matrix products, arithmetic and copies ran while one was open for 0% of the time, Pallas kernels for 0%

commit v1 on v0

v1 whole, which is shorter than its diff:
```python
import functools
import math

import jax
import jax.numpy as jnp
from jax import lax
from jax.experimental import pallas as pl
from jax.experimental.pallas import tpu as pltpu
from jax.sharding import PartitionSpec as P

ITERS = 2
CHUNK = 1024
SKEW = 2
MESH = pl.DeviceIdType.MESH


def kernel(
    sizes, frames_ref, slices_ref, prior_ref, orient_ref, out_ref,
    fv, sv, model, term, from_left, from_right, to_right, to_left,
    raws, counts, raw_acc, norm_acc, weights,
    frame_sem, slice_sem, right_send, right_recv, left_send, left_recv,
    raw_send, raw_recv, count_send, count_recv,
):
    n, panels, subs = sizes
    group = panels * subs
    z = lax.axis_index("frame")
    me = lax.axis_index("panel") * subs + lax.axis_index("sub")
    n_chunks, n_frames, width = fv.shape
    owned = slices_ref.shape[0]
    rows = model.shape[1]
    temper = 3.0 / math.sqrt(n_chunks * width * group)
    right, left = lax.rem(z + 1, n), lax.rem(z + n - 1, n)
    first, last = z == 0, z == n - 1

    slice_copy = pltpu.make_async_copy(slices_ref, sv, slice_sem)
    slice_copy.start()

    def frame_copy(c):
        start = pl.multiple_of(c * width, width)
        return pltpu.make_async_copy(frames_ref.at[:, pl.ds(start, width)], fv.at[c], frame_sem.at[c])

    @pl.loop(0, n_chunks)
    def _(c):
        frame_copy(c).start()

    def group_peer(k):
        other = lax.rem(me + k, group)
        return {"panel": other // subs, "sub": lax.rem(other, subs)}

    def frame_peer(k):
        return {"frame": lax.rem(z + k, n)}

    barrier = pltpu.get_barrier_semaphore()
    for k in range(1, group):
        pl.semaphore_signal(barrier, inc=1, device_id=group_peer(k), device_id_type=MESH)
    for k in range(1, n):
        pl.semaphore_signal(barrier, inc=1, device_id=frame_peer(k), device_id_type=MESH)

    slice_copy.wait()
    row = lax.broadcasted_iota(jnp.int32, (rows, 1), 0)
    prior = lax.fori_loop(
        0, rows, lambda m, v: jnp.where(row == m, prior_ref[orient_ref[m]], v), jnp.zeros((rows, 1), jnp.float32)
    )

    pl.semaphore_wait(barrier, group + n - 2)

    def right_copy(p, c):
        return pltpu.make_async_remote_copy(
            to_right.at[p, c], from_left.at[p, c], right_send.at[p, c], right_recv.at[p, c],
            device_id={"frame": right}, device_id_type=MESH,
        )

    def left_copy(p, c):
        return pltpu.make_async_remote_copy(
            to_left.at[p, c], from_right.at[p, c], left_send.at[p, c], left_recv.at[p, c],
            device_id={"frame": left}, device_id_type=MESH,
        )

    def raw_copy(it, k, slot):
        return pltpu.make_async_remote_copy(
            raws.at[it, me], raws.at[it, slot], raw_send.at[it, k], raw_recv.at[it, slot],
            device_id=group_peer(k), device_id_type=MESH,
        )

    def count_copy(it, k, slot):
        return pltpu.make_async_remote_copy(
            counts.at[it, z], counts.at[it, slot], count_send.at[it, k], count_recv.at[it, slot],
            device_id=frame_peer(k), device_id_type=MESH,
        )

    def sweep(p, make_term, combine):
        def step(s, _):
            @pl.when(s < n_chunks)
            def _():
                term[s] = make_term(s)

            c_right = s - z * SKEW

            @pl.when((c_right >= 0) & (c_right < n_chunks))
            def _():
                @pl.when(z > 0)
                def _():
                    right_copy(p, c_right).wait_recv()

                @pl.when(z < n - 1)
                def _():
                    came = jnp.where(first, 0.0, from_left[p, c_right].astype(jnp.float32))
                    to_right[p, c_right] = (came + term[c_right].astype(jnp.float32)).astype(jnp.bfloat16)
                    right_copy(p, c_right).start()

            c_left = s - (n - 1 - z) * SKEW

            @pl.when((c_left >= 0) & (c_left < n_chunks))
            def _():
                @pl.when(z < n - 1)
                def _():
                    left_copy(p, c_left).wait_recv()

                @pl.when(z > 0)
                def _():
                    came = jnp.where(last, 0.0, from_right[p, c_left].astype(jnp.float32))
                    to_left[p, c_left] = (came + term[c_left].astype(jnp.float32)).astype(jnp.bfloat16)
                    left_copy(p, c_left).start()

            c = s - jnp.maximum(z, n - 1 - z) * SKEW

            @pl.when((c >= 0) & (c < n_chunks))
            def _():
                low = jnp.where(first, 0.0, from_left[p, c].astype(jnp.float32))
                high = jnp.where(last, 0.0, from_right[p, c].astype(jnp.float32))
                combine(c, low + term[c].astype(jnp.float32) + high)

            return 0

        lax.fori_loop(0, n_chunks + (n - 1) * SKEW, step, 0)

    def score(c, rounded):
        model[c] = rounded
        wide = rounded.astype(jnp.float32)
        norm_acc[...] += jnp.sum(wide * wide, axis=1, keepdims=True)
        raw_acc[...] += lax.dot_general(
            rounded, fv[c], (((1,), (1,)), ((), ())), preferred_element_type=jnp.float32
        )

    def clear():
        raw_acc[...] = jnp.zeros_like(raw_acc)
        norm_acc[...] = jnp.zeros_like(norm_acc)

    def expect(it):
        raws[it, me] = raw_acc[...] - 0.5 * norm_acc[...]
        for k in range(1, group):
            raw_copy(it, k, me).start()
        for k in range(1, group):
            raw_copy(it, k, lax.rem(me + group - k, group)).wait_recv()
        summed = raws[it, 0]
        for j in range(1, group):
            summed = summed + raws[it, j]
        scores = temper * summed + prior
        top = jnp.exp(scores - jnp.max(scores, axis=0, keepdims=True))
        w = (top / jnp.sum(top, axis=0, keepdims=True)).astype(jnp.bfloat16)
        weights[...] = w
        mine = jnp.sum(w.astype(jnp.float32), axis=1, keepdims=True)
        counts[it, z] = jnp.broadcast_to(mine, counts.shape[2:])

        @pl.loop(1, n)
        def _(k):
            count_copy(it, k, z).start()

    def total_counts(it):
        @pl.loop(1, n)
        def _(k):
            count_copy(it, k, lax.rem(z + n - k, n)).wait_recv()

        total = lax.fori_loop(1, n, lambda j, v: v + counts[it, j], counts[it, 0])
        return total[:, :1]

    def weighted(c):
        return jnp.dot(weights[...], fv[c], preferred_element_type=jnp.float32).astype(jnp.bfloat16)

    def placed(c):
        own = sv[:, pl.ds(pl.multiple_of(c * width, width), width)]
        return jnp.where(row // owned == z, jnp.concatenate([own] * n, axis=0), 0.0).astype(jnp.bfloat16)

    def picked(values):
        parts = [values[o * owned : (o + 1) * owned] for o in range(n)]
        return functools.reduce(lambda a, o: jnp.where(z == o, parts[o], a), range(1, n), parts[0])

    def combine_first(c, total):
        frame_copy(c).wait()
        score(c, total.astype(jnp.bfloat16))

    clear()
    sweep(0, placed, combine_first)
    for it in range(ITERS):
        expect(it)
        divisor = total_counts(it) + 1.0
        if it + 1 < ITERS:
            clear()

            def combine_next(c, total):
                score(c, ((total + model[c].astype(jnp.float32)) / divisor).astype(jnp.bfloat16))

            sweep(it + 1, weighted, combine_next)
        else:

            def combine_last(c, total):
                start = pl.multiple_of(c * width, width)
                new = (total + model[c].astype(jnp.float32)) / divisor
                out_ref[:, pl.ds(start, width)] = picked(new)

            sweep(it + 1, weighted, combine_last)

    for p in range(ITERS + 1):
        @pl.loop(0, n_chunks)
        def _(c):
            @pl.when(z < n - 1)
            def _():
                right_copy(p, c).wait_send()

            @pl.when(z > 0)
            def _():
                left_copy(p, c).wait_send()

    for it in range(ITERS):
        for k in range(1, group):
            raw_copy(it, k, me).wait_send()

        @pl.loop(1, n)
        def _(k):
            count_copy(it, k, z).wait_send()


def local(sizes, frames, slices, log_prior, orient):
    n, panels, subs = sizes
    group = panels * subs
    n_frames, pixels = frames.shape
    owned = slices.shape[0]
    rows = n * owned
    width = min(CHUNK, pixels)
    chunks = pixels // width
    passes = ITERS + 1
    bf, f32 = jnp.bfloat16, jnp.float32
    dma = pltpu.SemaphoreType.DMA
    return pl.pallas_call(
        functools.partial(kernel, sizes),
        out_shape=jax.ShapeDtypeStruct((owned, pixels), f32),
        in_specs=[
            pl.BlockSpec(memory_space=pl.ANY),
            pl.BlockSpec(memory_space=pl.ANY),
            pl.BlockSpec(memory_space=pltpu.SMEM),
            pl.BlockSpec(memory_space=pltpu.SMEM),
        ],
        out_specs=pl.BlockSpec(memory_space=pltpu.VMEM),
        scratch_shapes=[
            pltpu.VMEM((chunks, n_frames, width), bf),
            pltpu.VMEM((owned, pixels), f32),
            pltpu.VMEM((chunks, rows, width), bf),
            pltpu.VMEM((chunks, rows, width), bf),
            pltpu.VMEM((passes, chunks, rows, width), bf),
            pltpu.VMEM((passes, chunks, rows, width), bf),
            pltpu.VMEM((passes, chunks, rows, width), bf),
            pltpu.VMEM((passes, chunks, rows, width), bf),
            pltpu.VMEM((ITERS, group, rows, n_frames), f32),
            pltpu.VMEM((ITERS, n, rows, 128), f32),
            pltpu.VMEM((rows, n_frames), f32),
            pltpu.VMEM((rows, 1), f32),
            pltpu.VMEM((rows, n_frames), bf),
            dma((chunks,)),
            dma,
            dma((passes, chunks)),
            dma((passes, chunks)),
            dma((passes, chunks)),
            dma((passes, chunks)),
            dma((ITERS, group)),
            dma((ITERS, group)),
            dma((ITERS, n)),
            dma((ITERS, n)),
        ],
        compiler_params=pltpu.CompilerParams(
            collective_id=0, has_side_effects=True, vmem_limit_bytes=56 * 1024 * 1024
        ),
    )(frames, slices, log_prior, orient)


def solution(mesh):
    in_specs = (
        P(("groups", "frame"), ("panel", "sub")),
        P(("groups", "frame"), ("panel", "sub")),
        P(),
        P("groups"),
    )
    out_specs = P(("groups", "frame"), ("panel", "sub"))
    sizes = (mesh.shape["frame"], mesh.shape["panel"], mesh.shape["sub"])
    return jax.shard_map(
        functools.partial(local, sizes), mesh=mesh, in_specs=in_specs, out_specs=out_specs, check_vma=False
    )
```

time: 174 us -> 115 us (0.66)
  Pallas kernels: 0 us -> 113 us
  blocking collectives: 77.1 us -> 0 us
  waiting for transfers between devices: 54.2 us -> 0 us
  matrix products: 22.2 us -> 0 us
  between operations: 14.1 us -> 0.01 us
  other arithmetic: 5.48 us -> 0 us
    pallas_call x0 -> x1, Pallas kernels: none -> 113 us  [local(): pl.pallas_call(functools.partial(kernel, sizes), out_shape=jax.ShapeDtype...]
    unnamed x4 -> x0, waiting for transfers between devices: 54.2 us -> none
    psum x4 -> x0, blocking collectives: 43.6 us -> none  [the longest x2 23.3 us: local(): counts = lax.psum(jnp.sum(weights.astype(jnp.float32), axis=0), 'frame')]
    all_gather x2 -> x0, blocking collectives: 33.5 us -> none  [fetch_slices(): return lax.all_gather(owned_b, 'frame', axis=0, tiled=True)]
    dot_general x4 -> x0, matrix products: 22.2 us -> none  [the longest x2 11.3 us: local(): jnp.einsum('fp,mp->fm', frames, gathered, preferred_element_type=jnp.floa...]
    div x1 -> x0, other arithmetic: 1.77 us -> none  [owner_update(): return (mine + owned_b.astype(jnp.float32)) / (my_counts + 1.0)[:, None]]
  transfers between devices with their start and end apart: 2 -> 0, of which waited for: 2 -> 0; matrix products, arithmetic and copies ran while one was open for 0% -> 0% of each run, Pallas kernels for 0% -> 0%
where the time goes in v1:
time: 115 us; the launch traced here: 114 us
  Pallas kernels  113 us (98%)
  local copies, waits for them, and re-layouts  1.67 us (1%)
    pallas_call x1, Pallas kernels, local(): pl.pallas_call(functools.partial(kernel, sizes), out_shape=jax.ShapeDtype...  113 us

profile of v1, /device:TPU:0, one launch (start us, length us, event | category | flops | bytes accessed | tf_op | source)
XLA Modules:
  0.0 114.3 jit_solution(9632575232092205592)
XLA Ops:
  0.0 112.6 %shard_map.46 = f32[4,16384]{1,0:T(4,128)} custom-call(bf16[256,16384]{1,0:T(8,128)(2,1)} %frames_ref.1, f32[4,16384]{1,0:T(4,128)} %slices_ref.1, f32[4096]{0:T(1024)} %prior_ref.1, s32[16]{0:T(128)} %orient_ref.1), custom_call_target="tpu_custom_call" | custom-call | tf_op jit(solution)/shard_map/pallas_call | solution.py:244
  112.6 1.7 %copy.6 = f32[4,16384]{1,0:T(4,128)} copy(f32[4,16384]{1,0:T(4,128)} %shard_map.46) | data formatting | bytes 524288

commit v2 on v1

--- a/solution.py
+++ b/solution.py
@@ -10,16 +10,17 @@
 
 ITERS = 2
 CHUNK = 1024
-SKEW = 2
+SKEW = 6
 MESH = pl.DeviceIdType.MESH
 
 
 def kernel(
     sizes, frames_ref, slices_ref, prior_ref, orient_ref, out_ref,
-    fv, sv, model, term, from_left, from_right, to_right, to_left,
-    raws, counts, raw_acc, norm_acc, weights,
+    fv, sv, model, gathered, sending, landed, term, from_left, from_right, to_right, to_left,
+    raws, counts, raw_acc, norm_acc, weights, divisor,
     frame_sem, slice_sem, right_send, right_recv, left_send, left_recv,
     raw_send, raw_recv, count_send, count_recv,
+    gather_send, gather_recv, owner_send, owner_recv,
 ):
     n, panels, subs = sizes
     group = panels * subs
@@ -28,6 +29,8 @@
     n_chunks, n_frames, width = fv.shape
     owned = slices_ref.shape[0]
     rows = model.shape[1]
+    groups, packed = gathered.shape[1:3]
+    fold = packed // owned
     temper = 3.0 / math.sqrt(n_chunks * width * group)
     right, left = lax.rem(z + 1, n), lax.rem(z + n - 1, n)
     first, last = z == 0, z == n - 1
@@ -172,45 +175,112 @@
             count_copy(it, k, lax.rem(z + n - k, n)).wait_recv()
 
         total = lax.fori_loop(1, n, lambda j, v: v + counts[it, j], counts[it, 0])
-        return total[:, :1]
+        divisor[...] = total[:, :1] + 1.0
 
     def weighted(c):
         return jnp.dot(weights[...], fv[c], preferred_element_type=jnp.float32).astype(jnp.bfloat16)
-
-    def placed(c):
-        own = sv[:, pl.ds(pl.multiple_of(c * width, width), width)]
-        return jnp.where(row // owned == z, jnp.concatenate([own] * n, axis=0), 0.0).astype(jnp.bfloat16)
 
     def picked(values):
         parts = [values[o * owned : (o + 1) * owned] for o in range(n)]
         return functools.reduce(lambda a, o: jnp.where(z == o, parts[o], a), range(1, n), parts[0])
 
-    def combine_first(c, total):
-        frame_copy(c).wait()
-        score(c, total.astype(jnp.bfloat16))
+    def columns(c):
+        return pl.ds(pl.multiple_of(c * width, width), width)
+
+    def gather_copy(g, k, slot):
+        return pltpu.make_async_remote_copy(
+            gathered.at[z, g], gathered.at[slot, g], gather_send.at[k, g], gather_recv.at[slot, g],
+            device_id=frame_peer(k), device_id_type=MESH,
+        )
+
+    def owner_copy(g, k, slot):
+        to = lax.rem(z + k, n)
+        return pltpu.make_async_remote_copy(
+            sending.at[to, g], landed.at[slot, g], owner_send.at[k, g], owner_recv.at[slot, g],
+            device_id={"frame": to}, device_id_type=MESH,
+        )
+
+    def source(k):
+        return lax.rem(z + n - k, n)
+
+    @pl.loop(0, groups)
+    def _(g):
+        own = [sv[:, columns(g * fold + j)] for j in range(fold)]
+        gathered[z, g] = jnp.concatenate(own, axis=0).astype(jnp.bfloat16)
+
+        @pl.loop(1, n)
+        def _(k):
+            gather_copy(g, k, z).start()
 
     clear()
-    sweep(0, placed, combine_first)
+
+    @pl.loop(0, groups)
+    def _(g):
+        @pl.loop(1, n)
+        def _(k):
+            gather_copy(g, k, source(k)).wait_recv()
+
+        blocks = [gathered[o, g].astype(jnp.float32) for o in range(n)]
+        for j in range(fold):
+            c = g * fold + j
+            frame_copy(c).wait()
+            whole = jnp.concatenate([b[j * owned : (j + 1) * owned] for b in blocks], axis=0)
+            score(c, whole.astype(jnp.bfloat16))
+
+    def last_update():
+        @pl.loop(0, groups)
+        def _(g):
+            terms = [
+                jnp.dot(weights[...], fv[g * fold + j], preferred_element_type=jnp.float32) for j in range(fold)
+            ]
+            for o in range(n):
+                part = [t[o * owned : (o + 1) * owned] for t in terms]
+                sending[o, g] = jnp.concatenate(part, axis=0).astype(jnp.bfloat16)
+
+            @pl.loop(1, n)
+            def _(k):
+                owner_copy(g, k, z).start()
+
+            landed[z, g] = sending[z, g]
+
+        count_total()
+        divide = jnp.concatenate([picked(divisor[...])] * fold, axis=0)
+
+        @pl.loop(0, groups)
+        def _(g):
+            @pl.loop(1, n)
+            def _(k):
+                owner_copy(g, k, source(k)).wait_recv()
+
+            own = [picked(model[g * fold + j].astype(jnp.float32)) for j in range(fold)]
+            total = landed[0, g].astype(jnp.float32)
+            for o in range(1, n):
+                total = total + landed[o, g].astype(jnp.float32)
+            new = (total + jnp.concatenate(own, axis=0)) / divide
+            for j in range(fold):
+                out_ref[:, columns(g * fold + j)] = new[j * owned : (j + 1) * owned]
+
     for it in range(ITERS):
         expect(it)
-        divisor = total_counts(it) + 1.0
+
+        def count_total():
+            total_counts(it)
+
         if it + 1 < ITERS:
             clear()
 
             def combine_next(c, total):
-                score(c, ((total + model[c].astype(jnp.float32)) / divisor).astype(jnp.bfloat16))
-
-            sweep(it + 1, weighted, combine_next)
+                @pl.when(c == 0)
+                def _():
+                    count_total()
+
+                score(c, ((total + model[c].astype(jnp.float32)) / divisor[...]).astype(jnp.bfloat16))
+
+            sweep(it, weighted, combine_next)
         else:
-
-            def combine_last(c, total):
-                start = pl.multiple_of(c * width, width)
-                new = (total + model[c].astype(jnp.float32)) / divisor
-                out_ref[:, pl.ds(start, width)] = picked(new)
-
-            sweep(it + 1, weighted, combine_last)
-
-    for p in range(ITERS + 1):
+            last_update()
+
+    for p in range(ITERS - 1):
         @pl.loop(0, n_chunks)
         def _(c):
             @pl.when(z < n - 1)
@@ -228,6 +298,13 @@
         @pl.loop(1, n)
         def _(k):
             count_copy(it, k, z).wait_send()
+
+    @pl.loop(0, groups)
+    def _(g):
+        @pl.loop(1, n)
+        def _(k):
+            gather_copy(g, k, z).wait_send()
+            owner_copy(g, k, z).wait_send()
 
 
 def local(sizes, frames, slices, log_prior, orient):
@@ -238,7 +315,10 @@
     rows = n * owned
     width = min(CHUNK, pixels)
     chunks = pixels // width
-    passes = ITERS + 1
+    passes = ITERS - 1
+    fold = max(1, 16 // owned)
+    groups = chunks // fold
+    block = (n, groups, fold * owned, width)
     bf, f32 = jnp.bfloat16, jnp.float32
     dma = pltpu.SemaphoreType.DMA
     return pl.pallas_call(
@@ -255,6 +335,9 @@
             pltpu.VMEM((chunks, n_frames, width), bf),
             pltpu.VMEM((owned, pixels), f32),
             pltpu.VMEM((chunks, rows, width), bf),
+            pltpu.VMEM(block, bf),
+            pltpu.VMEM(block, bf),
+            pltpu.VMEM(block, bf),
             pltpu.VMEM((chunks, rows, width), bf),
             pltpu.VMEM((passes, chunks, rows, width), bf),
             pltpu.VMEM((passes, chunks, rows, width), bf),
@@ -265,6 +348,7 @@
             pltpu.VMEM((rows, n_frames), f32),
             pltpu.VMEM((rows, 1), f32),
             pltpu.VMEM((rows, n_frames), bf),
+            pltpu.VMEM((rows, 1), f32),
             dma((chunks,)),
             dma,
             dma((passes, chunks)),
@@ -275,6 +359,10 @@
             dma((ITERS, group)),
             dma((ITERS, n)),
             dma((ITERS, n)),
+            dma((n, groups)),
+            dma((n, groups)),
+            dma((n, groups)),
+            dma((n, groups)),
         ],
         compiler_params=pltpu.CompilerParams(
             collective_id=0, has_side_effects=True, vmem_limit_bytes=56 * 1024 * 1024

time: 115 us -> 63.4 us (0.55)
  Pallas kernels: 113 us -> 61.5 us
    pallas_call x1, Pallas kernels: 113 us -> 61.5 us  [local(): pl.pallas_call(functools.partial(kernel, sizes), out_shape=jax.ShapeDtype...]
where the time goes in v2:
time: 63.4 us; the launch traced here: 63.2 us
  Pallas kernels  61.5 us (97%)
  local copies, waits for them, and re-layouts  1.67 us (3%)
    pallas_call x1, Pallas kernels, local(): pl.pallas_call(functools.partial(kernel, sizes), out_shape=jax.ShapeDtype...  61.5 us
    unnamed x1, local copies, waits for them, and re-layouts  1.67 us

profile of v2, /device:TPU:0, one launch (start us, length us, event | category | flops | bytes accessed | tf_op | source)
XLA Modules:
  0.0 63.2 jit_solution(9011048125073073292)
XLA Ops:
  0.0 61.5 %shard_map.46 = f32[4,16384]{1,0:T(4,128)} custom-call(bf16[256,16384]{1,0:T(8,128)(2,1)} %frames_ref.1, f32[4,16384]{1,0:T(4,128)} %slices_ref.1, f32[4096]{0:T(1024)} %prior_ref.1, s32[16]{0:T(128)} %orient_ref.1), custom_call_target="tpu_custom_call" | custom-call | tf_op jit(solution)/shard_map/pallas_call | solution.py:324
  61.5 1.7 %copy.6 = f32[4,16384]{1,0:T(4,128)} copy(f32[4,16384]{1,0:T(4,128)} %shard_map.46) | data formatting | bytes 524288

commit v3 on v2

--- a/solution.py
+++ b/solution.py
@@ -10,15 +10,16 @@
 
 ITERS = 2
 CHUNK = 1024
-SKEW = 6
+SKEW = 5
+PIECE = 1024
 MESH = pl.DeviceIdType.MESH
 
 
 def kernel(
-    sizes, frames_ref, slices_ref, prior_ref, orient_ref, out_ref,
-    fv, sv, model, gathered, sending, landed, term, from_left, from_right, to_right, to_left,
+    sizes, frames_ref, slices_ref, prior_hbm, orient_hbm, out_hbm,
+    fv, sv, prior_ref, orient_ref, out_ref, prior_col, model, gathered, sending, landed, term, from_left, from_right, to_right, to_left,
     raws, counts, raw_acc, norm_acc, weights, divisor,
-    frame_sem, slice_sem, right_send, right_recv, left_send, left_recv,
+    frame_sem, slice_sem, prior_sem, orient_sem, out_sem, right_send, right_recv, left_send, left_recv,
     raw_send, raw_recv, count_send, count_recv,
     gather_send, gather_recv, owner_send, owner_recv,
 ):
@@ -29,7 +30,8 @@
     n_chunks, n_frames, width = fv.shape
     owned = slices_ref.shape[0]
     rows = model.shape[1]
-    groups, packed = gathered.shape[1:3]
+    groups, packed, piece = gathered.shape[1:]
+    split = width // piece
     fold = packed // owned
     temper = 3.0 / math.sqrt(n_chunks * width * group)
     right, left = lax.rem(z + 1, n), lax.rem(z + n - 1, n)
@@ -37,6 +39,10 @@
 
     slice_copy = pltpu.make_async_copy(slices_ref, sv, slice_sem)
     slice_copy.start()
+    prior_copy = pltpu.make_async_copy(prior_hbm, prior_ref, prior_sem)
+    prior_copy.start()
+    orient_copy = pltpu.make_async_copy(orient_hbm, orient_ref, orient_sem)
+    orient_copy.start()
 
     def frame_copy(c):
         start = pl.multiple_of(c * width, width)
@@ -59,11 +65,18 @@
     for k in range(1, n):
         pl.semaphore_signal(barrier, inc=1, device_id=frame_peer(k), device_id_type=MESH)
 
+    def group_columns(g, j):
+        return pl.ds(pl.multiple_of(g * (fold * piece) + j * piece, piece), piece)
+
+    def part_frames(g, j):
+        return fv[g * fold // split + j // split, :, j % split * piece : (j % split + 1) * piece]
+
     slice_copy.wait()
-    row = lax.broadcasted_iota(jnp.int32, (rows, 1), 0)
-    prior = lax.fori_loop(
-        0, rows, lambda m, v: jnp.where(row == m, prior_ref[orient_ref[m]], v), jnp.zeros((rows, 1), jnp.float32)
-    )
+
+    @pl.loop(0, groups)
+    def _(g):
+        own = [sv[:, group_columns(g, j)] for j in range(fold)]
+        gathered[z, g] = jnp.concatenate(own, axis=0).astype(jnp.bfloat16)
 
     pl.semaphore_wait(barrier, group + n - 2)
 
@@ -137,12 +150,11 @@
 
         lax.fori_loop(0, n_chunks + (n - 1) * SKEW, step, 0)
 
-    def score(c, rounded):
-        model[c] = rounded
+    def score(rounded, frames):
         wide = rounded.astype(jnp.float32)
         norm_acc[...] += jnp.sum(wide * wide, axis=1, keepdims=True)
         raw_acc[...] += lax.dot_general(
-            rounded, fv[c], (((1,), (1,)), ((), ())), preferred_element_type=jnp.float32
+            rounded, frames, (((1,), (1,)), ((), ())), preferred_element_type=jnp.float32
         )
 
     def clear():
@@ -158,7 +170,7 @@
         summed = raws[it, 0]
         for j in range(1, group):
             summed = summed + raws[it, j]
-        scores = temper * summed + prior
+        scores = temper * summed + prior_col[...]
         top = jnp.exp(scores - jnp.max(scores, axis=0, keepdims=True))
         w = (top / jnp.sum(top, axis=0, keepdims=True)).astype(jnp.bfloat16)
         weights[...] = w
@@ -184,9 +196,6 @@
         parts = [values[o * owned : (o + 1) * owned] for o in range(n)]
         return functools.reduce(lambda a, o: jnp.where(z == o, parts[o], a), range(1, n), parts[0])
 
-    def columns(c):
-        return pl.ds(pl.multiple_of(c * width, width), width)
-
     def gather_copy(g, k, slot):
         return pltpu.make_async_remote_copy(
             gathered.at[z, g], gathered.at[slot, g], gather_send.at[k, g], gather_recv.at[slot, g],
@@ -205,14 +214,17 @@
 
     @pl.loop(0, groups)
     def _(g):
-        own = [sv[:, columns(g * fold + j)] for j in range(fold)]
-        gathered[z, g] = jnp.concatenate(own, axis=0).astype(jnp.bfloat16)
-
         @pl.loop(1, n)
         def _(k):
             gather_copy(g, k, z).start()
 
     clear()
+    prior_copy.wait()
+    orient_copy.wait()
+    row = lax.broadcasted_iota(jnp.int32, (rows, 1), 0)
+    prior_col[...] = lax.fori_loop(
+        0, rows, lambda m, v: jnp.where(row == m, prior_ref[orient_ref[m]], v), jnp.zeros((rows, 1), jnp.float32)
+    )
 
     @pl.loop(0, groups)
     def _(g):
@@ -221,17 +233,22 @@
             gather_copy(g, k, source(k)).wait_recv()
 
         blocks = [gathered[o, g].astype(jnp.float32) for o in range(n)]
+        for j in range(fold // split):
+            frame_copy(g * fold // split + j).wait()
         for j in range(fold):
-            c = g * fold + j
-            frame_copy(c).wait()
-            whole = jnp.concatenate([b[j * owned : (j + 1) * owned] for b in blocks], axis=0)
-            score(c, whole.astype(jnp.bfloat16))
+            whole = jnp.concatenate([b[j * owned : (j + 1) * owned] for b in blocks], axis=0).astype(jnp.bfloat16)
+            model[g * fold // split + j // split, :, j % split * piece : (j % split + 1) * piece] = whole
+            score(whole, part_frames(g, j))
+
+    def out_copy(g):
+        span = pl.ds(pl.multiple_of(g * (fold * piece), fold * piece), fold * piece)
+        return pltpu.make_async_copy(out_ref.at[:, span], out_hbm.at[:, span], out_sem.at[g])
 
     def last_update():
         @pl.loop(0, groups)
         def _(g):
             terms = [
-                jnp.dot(weights[...], fv[g * fold + j], preferred_element_type=jnp.float32) for j in range(fold)
+                jnp.dot(weights[...], part_frames(g, j), preferred_element_type=jnp.float32) for j in range(fold)
             ]
             for o in range(n):
                 part = [t[o * owned : (o + 1) * owned] for t in terms]
@@ -252,13 +269,22 @@
             def _(k):
                 owner_copy(g, k, source(k)).wait_recv()
 
-            own = [picked(model[g * fold + j].astype(jnp.float32)) for j in range(fold)]
+            held = [model[g * fold // split + c] for c in range(fold // split)]
+            own = [
+                picked(held[j // split][:, j % split * piece : (j % split + 1) * piece].astype(jnp.float32))
+                for j in range(fold)
+            ]
             total = landed[0, g].astype(jnp.float32)
             for o in range(1, n):
                 total = total + landed[o, g].astype(jnp.float32)
             new = (total + jnp.concatenate(own, axis=0)) / divide
             for j in range(fold):
-                out_ref[:, columns(g * fold + j)] = new[j * owned : (j + 1) * owned]
+                out_ref[:, group_columns(g, j)] = new[j * owned : (j + 1) * owned]
+            out_copy(g).start()
+
+        @pl.loop(0, groups)
+        def _(g):
+            out_copy(g).wait()
 
     for it in range(ITERS):
         expect(it)
@@ -274,7 +300,9 @@
                 def _():
                     count_total()
 
-                score(c, ((total + model[c].astype(jnp.float32)) / divisor[...]).astype(jnp.bfloat16))
+                rounded = ((total + model[c].astype(jnp.float32)) / divisor[...]).astype(jnp.bfloat16)
+                model[c] = rounded
+                score(rounded, fv[c])
 
             sweep(it, weighted, combine_next)
         else:
@@ -317,8 +345,9 @@
     chunks = pixels // width
     passes = ITERS - 1
     fold = max(1, 16 // owned)
-    groups = chunks // fold
-    block = (n, groups, fold * owned, width)
+    piece = min(PIECE, width)
+    groups = pixels // (fold * piece)
+    block = (n, groups, fold * owned, piece)
     bf, f32 = jnp.bfloat16, jnp.float32
     dma = pltpu.SemaphoreType.DMA
     return pl.pallas_call(
@@ -327,13 +356,17 @@
         in_specs=[
             pl.BlockSpec(memory_space=pl.ANY),
             pl.BlockSpec(memory_space=pl.ANY),
-            pl.BlockSpec(memory_space=pltpu.SMEM),
-            pl.BlockSpec(memory_space=pltpu.SMEM),
+            pl.BlockSpec(memory_space=pl.ANY),
+            pl.BlockSpec(memory_space=pl.ANY),
         ],
-        out_specs=pl.BlockSpec(memory_space=pltpu.VMEM),
+        out_specs=pl.BlockSpec(memory_space=pl.ANY),
         scratch_shapes=[
             pltpu.VMEM((chunks, n_frames, width), bf),
             pltpu.VMEM((owned, pixels), f32),
+            pltpu.SMEM(log_prior.shape, f32),
+            pltpu.SMEM(orient.shape, jnp.int32),
+            pltpu.VMEM((owned, pixels), f32),
+            pltpu.VMEM((rows, 1), f32),
             pltpu.VMEM((chunks, rows, width), bf),
             pltpu.VMEM(block, bf),
             pltpu.VMEM(block, bf),
@@ -351,6 +384,9 @@
             pltpu.VMEM((rows, 1), f32),
             dma((chunks,)),
             dma,
+            dma,
+            dma,
+            dma((groups,)),
             dma((passes, chunks)),
             dma((passes, chunks)),
             dma((passes, chunks)),

time: 63.4 us -> 60 us (0.946)
  Pallas kernels: 61.5 us -> 58.2 us
    pallas_call x1, Pallas kernels: 61.5 us -> 58.2 us  [local(): pl.pallas_call(functools.partial(kernel, sizes), out_shape=jax.ShapeDtype...]
where the time goes in v3:
time: 60 us; the launch traced here: 59.9 us
  Pallas kernels  58.2 us (97%)
  local copies, waits for them, and re-layouts  1.67 us (3%)
    pallas_call x1, Pallas kernels, local(): pl.pallas_call(functools.partial(kernel, sizes), out_shape=jax.ShapeDtype...  58.2 us
    unnamed x1, local copies, waits for them, and re-layouts  1.67 us

profile of v3, /device:TPU:0, one launch (start us, length us, event | category | flops | bytes accessed | tf_op | source)
XLA Modules:
  0.0 59.9 jit_solution(8689823441524652465)
XLA Ops:
  0.0 58.2 %shard_map.46 = f32[4,16384]{1,0:T(4,128)} custom-call(bf16[256,16384]{1,0:T(8,128)(2,1)} %frames_ref.1, f32[4,16384]{1,0:T(4,128)} %slices_ref.1, f32[4096]{0:T(1024)} %prior_hbm.1, s32[16]{0:T(128)} %orient_hbm.1), custom_call_target="tpu_custom_call" | custom-call | tf_op jit(solution)/shard_map/pallas_call | solution.py:353
  58.2 1.7 %copy.6 = f32[4,16384]{1,0:T(4,128)} copy(f32[4,16384]{1,0:T(4,128)} %shard_map.46) | data formatting | bytes 524288
